TPU v7x, 32 devices: a whole 2x2x4 slice. The times are simulated.
32 devices in a mesh: row: 4 (over y, core), col: 8 (over z, x).
Axes of the slice: x: 2, y: 2, z: 4, core: 2. Of those that a mesh axis runs over, the one named last changes fastest.
Arguments:
- factor: float32 [6, 2048, 6, 2048], P(None, 'row', None, 'col'), may hold values from -0.0625 to 0.0625
- diag_inv: float32 [6, 2048, 2048], P(None, None, 'row'), may hold values from -2 to 2, as said below
- structure: int32 [6, 6, 16], P(None, None, 'row'), may hold values 0 or 1
- parent: int32 [6], replicated, may hold values from 1 to 6, as said below
- post: float32 [6, 2048, 64], P(None, 'row', 'col'), may hold values from -6 to 6
Outputs:
- mean_x: float32 [6, 2048, 64], P(None, 'row', 'col')
- variance: float32 [6, 2048], P(None, 'row')
Inputs may be any that keep to these rules, and one draw needn't show every extreme that they name: parent[s] > s for s < 5, and parent[5] = 6; every supernode has at most 2 ancestors, and some supernode has exactly that many. The diagonal of each diag_inv[s] lies in 0.5 to 2.
All inputs are finite; a program needn't handle non-finite values. No bound on the sum of `structure` on one device may be relied on, other than what follows from the above.
Results may differ from a plain program's by a relative error of at most 0.00014.
Values sent between devices are 32-bit elements; how exact they have to be, the bound alone decides.
A program may use at most 192 MiB of HBM per device.

v0:
```python
import jax
import jax.numpy as jnp
from jax import lax
from jax.sharding import PartitionSpec as P

LEVELS = 3
HIGHEST = lax.Precision.HIGHEST


def contract(selected, panel_piece):
    return jnp.einsum("tiw,tin->wn", panel_piece, selected, precision=HIGHEST)


def body(factor, diag_inv, structure, parent, post):
    super_count = factor.shape[0]
    row_width = factor.shape[1]
    col_width = factor.shape[3]
    full_width = diag_inv.shape[1]
    rhs_width = post.shape[2]
    row_at = lax.axis_index("row")
    col_at = lax.axis_index("col")
    extended = jnp.concatenate([parent, jnp.full((1,), super_count, jnp.int32)])
    slot_ids = jnp.arange(super_count + 1, dtype=jnp.int32)
    targets = jnp.arange(super_count, dtype=jnp.int32)
    ancestor_hops = []
    current = parent
    for hop_index in range(super_count - 1):
        ancestor_hops.append(current)
        onehot = (current[:, None] == slot_ids[None, :]).astype(jnp.int32)
        current = jnp.sum(onehot * extended[None, :], axis=1)
    ancestry = jnp.zeros((super_count, super_count), jnp.float32)
    for hop_targets in ancestor_hops:
        ancestry = ancestry + (hop_targets[:, None] == targets[None, :]).astype(jnp.float32)
    block_rows = row_width // structure.shape[2]
    row_mask = jnp.repeat(structure.astype(jnp.float32), block_rows, axis=2) * ancestry[:, :, None]
    masked = factor * jnp.transpose(row_mask, (1, 2, 0))[:, :, :, None]
    rows_full = jnp.arange(full_width, dtype=jnp.int32)
    own_cols = row_at * row_width + jnp.arange(row_width, dtype=jnp.int32)
    lower_inv = jnp.where((rows_full[:, None] >= own_cols[None, :])[None, :, :], diag_inv, 0.0)
    unit_cols = col_at * col_width + jnp.arange(col_width, dtype=jnp.int32)
    unit_block = (rows_full[:, None] == unit_cols[None, :]).astype(jnp.float32)
    gathered = lax.all_gather(post, "row", axis=1, tiled=True)
    total_cols = super_count * col_width + rhs_width
    solution = jnp.zeros((super_count, row_width, total_cols), jnp.float32)
    for current_sup in range(super_count - 1, -1, -1):
        later_cols = (current_sup + 1) * col_width
        if current_sup == super_count - 1:
            summed = jnp.zeros((full_width, rhs_width), jnp.float32)
        else:
            picks = []
            chosen_rows = []
            for slot_index in range(LEVELS - 1):
                target = ancestor_hops[slot_index][current_sup]
                is_valid = (target < super_count).astype(jnp.float32)
                clamped = jnp.minimum(target, super_count - 1)
                picks.append(
                    lax.dynamic_index_in_dim(
                        masked[:, :, current_sup, :], clamped, 0, keepdims=False
                    )
                    * is_valid
                )
                chosen_rows.append(
                    lax.dynamic_index_in_dim(solution, clamped, 0, keepdims=False)[:, later_cols:]
                )
            blocks = jnp.stack(picks)
            selected = jnp.stack(chosen_rows)
            partial_value = contract(selected, lax.all_gather(blocks, "col", axis=2, tiled=True))
            summed = lax.psum(partial_value, "row")
        split_at = summed.shape[1] - rhs_width
        remaining = jnp.concatenate(
            [-summed[:, :split_at], gathered[current_sup] - summed[:, split_at:]], axis=1
        )
        right = jnp.concatenate([unit_block, remaining], axis=1)
        fresh = jnp.dot(
            lower_inv[current_sup].T, right, precision=HIGHEST, preferred_element_type=jnp.float32
        )
        solution = solution.at[current_sup, :, current_sup * col_width :].set(fresh)
    mean_x = solution[:, :, super_count * col_width :]
    unit_part = solution[:, :, : super_count * col_width]
    squares = jnp.sum(unit_part * unit_part, axis=2)
    variance = lax.psum(squares, "col")
    return (mean_x, variance)


def solution(mesh):
    return jax.shard_map(
        body,
        mesh=mesh,
        in_specs=(
            P(None, "row", None, "col"),
            P(None, None, "row"),
            P(None, None, "row"),
            P(),
            P(None, "row", "col"),
        ),
        out_specs=(P(None, "row", "col"), P(None, "row")),
        check_vma=False,
    )
```

profile of v0, /device:TPU:0, one launch (start us, length us, event | category | flops | bytes accessed | tf_op | source)
XLA Modules:
  0.0 1485.7 jit_solution(14807575500122001028)
XLA Ops:
  15.8 15.3 %broadcast_multiply_fusion = f32[6,512,6,256]{3,1,2,0:T(8,128)} fusion(f32[6,512,6,256]{3,1,2,0:T(8,128)} %param.17, f32[6,512,6]{1,2,0:T(8,128)S(1)} %multiply_bitcast_fusion.10), kind=kLoop, calls=%fused_computation.18 | loop fusion | flops 4718592 | bytes 37822464 | tf_op jit(solution)/shard_map/mul | solution.py:36
  31.1 10.7 fusion.93
  53.4 10.7 broadcast_select_fusion
  78.6 92.2 %all-gather.6.cloned.1.call-done = f32[2,512,2048]{2,1,0:T(8,128)} async-done(((f32[2,512,256]{2,1,0:T(8,128)}), f32[2,512,2048]{2,1,0:T(8,128)}) %all-gather.6.cloned.1.call-update) | async-done | bytes 8388624 | tf_op jit(solution)/shard_map/all_gather | solution.py:67
  170.8 11.2 convolution_bitcast_fusion.4
  199.4 33.4 %all-reduce.7.cloned.1.call-done = f32[2048,264]{0,1:T(8,128)} async-done(((f32[2048,264]{0,1:T(8,128)}), f32[2048,264]{0,1:T(8,128)}) %all-reduce.7.cloned.1.call-update) | async-done | bytes 2162704 | tf_op jit(solution)/shard_map/psum | solution.py:68
  235.5 9.8 fusion.73
  251.2 108.7 %all-gather.8.cloned.1.call-done = f32[2,512,2048]{2,1,0:T(8,128)} async-done(((f32[2,512,256]{2,1,0:T(8,128)}), f32[2,512,2048]{2,1,0:T(8,128)}) %all-gather.8.cloned.1.call-update) | async-done | bytes 8388624 | tf_op jit(solution)/shard_map/all_gather | solution.py:67
  359.9 18.0 %convolution_bitcast_fusion.3 = f32[2048,520]{0,1:T(8,128)} fusion(f32[2,512,2048]{2,1,0:T(8,128)} %all-gather.8.cloned.1.call-done, f32[1,512,520]{1,2,0:T(8,128)} %slice_bitcast_fusion.38, f32[1,512,520]{1,2,0:T(8,128)} %slice_bitcast_fusion.39), kind=kOutput, calls=%fused_computation.57 | convolution fusion | flops 13086760960 | bytes 14778368 | tf_op jit(solution)/shard_map/tiw,tin->wn/dot_general | solution.py:11
  380.1 82.8 %all-reduce.9.cloned.1.call-done = f32[2048,520]{0,1:T(8,128)} async-done(((f32[2048,520]{0,1:T(8,128)}), f32[2048,520]{0,1:T(8,128)}) %all-reduce.9.cloned.1.call-update) | async-done | bytes 4259856 | tf_op jit(solution)/shard_map/psum | solution.py:68
  466.3 13.2 bitcast_dynamic-update-slice_fusion
  485.7 104.2 %all-gather.10.cloned.1.call-done = f32[2,512,2048]{2,1,0:T(8,128)} async-done(((f32[2,512,256]{2,1,0:T(8,128)}), f32[2,512,2048]{2,1,0:T(8,128)}) %all-gather.10.cloned.1.call-update) | async-done | bytes 8388624 | tf_op jit(solution)/shard_map/all_gather | solution.py:67
  589.9 25.4 %convolution_bitcast_fusion.2 = f32[2048,776]{0,1:T(8,128)} fusion(f32[2,512,2048]{2,1,0:T(8,128)} %all-gather.10.cloned.1.call-done, f32[1,512,776]{1,2,0:T(8,128)} %slice_bitcast_fusion.28, f32[1,512,776]{1,2,0:T(8,128)} %slice_bitcast_fusion.29), kind=kOutput, calls=%fused_computation.56 | convolution fusion | flops 19529474048 | bytes 17924096 | tf_op jit(solution)/shard_map/tiw,tin->wn/dot_general | solution.py:11
  623.3 111.1 %all-reduce.11.cloned.1.call-done = f32[2048,776]{0,1:T(8,128)} async-done(((f32[2048,776]{0,1:T(8,128)}), f32[2048,776]{0,1:T(8,128)}) %all-reduce.11.cloned.1.call-update) | async-done | bytes 6357008 | tf_op jit(solution)/shard_map/psum | solution.py:68
  738.6 17.0 %fusion.53 = f32[6,512,1544]{1,2,0:T(8,128)} fusion(f32[6,512,1544]{1,2,0:T(8,128)} %bitcast_dynamic-update-slice_fusion, f32[2048,8]{0,1:T(8,128)S(1)} %slice_subtract_fusion.2, f32[2048,768]{0,1:T(8,128)S(1)} %slice_negate_fusion.2, f32[2048,256]{0,1:T(8,128)S(1)} %fusion.67, f32[6,2048,512]{2,1,0:T(8,128)} %copy-done), kind=kOutput, calls=%fused_computation.63 | convolution fusion | flops 12989792256 | bytes 14761984 | tf_op jit(solution)/shard_map/dot_general | solution.py:74
  762.1 99.4 %all-gather.12.cloned.1.call-done = f32[2,512,2048]{2,1,0:T(8,128)} async-done(((f32[2,512,256]{2,1,0:T(8,128)}), f32[2,512,2048]{2,1,0:T(8,128)}) %all-gather.12.cloned.1.call-update) | async-done | bytes 8388624 | tf_op jit(solution)/shard_map/all_gather | solution.py:67
  861.5 31.5 %convolution_bitcast_fusion.1 = f32[2048,1032]{0,1:T(8,128)} fusion(f32[2,512,2048]{2,1,0:T(8,128)} %all-gather.12.cloned.1.call-done, f32[1,512,1032]{1,2,0:T(8,128)} %slice_bitcast_fusion.26, f32[1,512,1032]{1,2,0:T(8,128)} %slice_bitcast_fusion.27), kind=kOutput, calls=%fused_computation.20 | convolution fusion | flops 25972187136 | bytes 21069824 | tf_op jit(solution)/shard_map/tiw,tin->wn/dot_general | solution.py:11
  894.4 150.9 %all-reduce.13.cloned.1.call-done = f32[2048,1032]{0,1:T(8,128)} async-done(((f32[2048,1032]{0,1:T(8,128)}), f32[2048,1032]{0,1:T(8,128)}) %all-reduce.13.cloned.1.call-update) | async-done | bytes 8454160 | tf_op jit(solution)/shard_map/psum | solution.py:68
  1050.4 20.4 %fusion.41 = f32[6,512,1544]{1,2,0:T(8,128)} fusion(f32[6,512,1544]{1,2,0:T(8,128)} %fusion.53, f32[2048,8]{0,1:T(8,128)S(1)} %slice_subtract_fusion.1, f32[2048,1024]{0,1:T(8,128)S(1)} %slice_negate_fusion.1, f32[2048,256]{0,1:T(8,128)S(1)} %fusion.67, f32[6,2048,512]{2,1,0:T(8,128)} %copy-done), kind=kOutput, calls=%fused_computation.59 | convolution fusion | flops 16212066304 | bytes 17383424 | tf_op jit(solution)/shard_map/dot_general | solution.py:74
  1077.9 94.5 %all-gather.14.cloned.1.call-done = f32[2,512,2048]{2,1,0:T(8,128)} async-done(((f32[2,512,256]{2,1,0:T(8,128)}), f32[2,512,2048]{2,1,0:T(8,128)}) %all-gather.14.cloned.1.call-update) | async-done | bytes 8388624 | tf_op jit(solution)/shard_map/all_gather | solution.py:67
  1172.5 42.1 %convolution_bitcast_fusion = f32[2048,1288]{0,1:T(8,128)} fusion(f32[2,512,2048]{2,1,0:T(8,128)} %all-gather.14.cloned.1.call-done, f32[1,512,1288]{1,2,0:T(8,128)} %slice_bitcast_fusion.24, f32[1,512,1288]{1,2,0:T(8,128)} %slice_bitcast_fusion.25), kind=kOutput, calls=%fused_computation.19 | convolution fusion | flops 32414900224 | bytes 24215552 | tf_op jit(solution)/shard_map/tiw,tin->wn/dot_general | solution.py:11
  1214.6 186.2 %all-reduce.15.cloned.1.call-done = f32[2048,1288]{0,1:T(8,128)} async-done(((f32[2048,1288]{0,1:T(8,128)}), f32[2048,1288]{0,1:T(8,128)}) %all-reduce.15.cloned.1.call-update) | async-done | bytes 10551312 | tf_op jit(solution)/shard_map/psum | solution.py:68
  1406.7 23.9 %fusion.47 = f32[6,512,1544]{1,2,0:T(8,128)} fusion(f32[6,512,1544]{1,2,0:T(8,128)} %fusion.41, f32[2048,8]{0,1:T(8,128)S(1)} %slice_subtract_fusion, f32[2048,1280]{0,1:T(8,128)S(1)} %slice_negate_fusion, f32[2048,256]{0,1:T(8,128)S(1)} %fusion.67, f32[6,2048,512]{2,1,0:T(8,128)} %copy-done), kind=kOutput, calls=%fused_computation.61 | convolution fusion | flops 19434340352 | bytes 20004864 | tf_op jit(solution)/shard_map/dot_general | solution.py:74
  1440.9 37.7 %psum.47 = f32[6,512]{1,0:T(8,128)} all-reduce(f32[6,512]{1,0:T(8,128)S(1)} %fusion), channel_id=1, replica_groups=mesh['row'=4,'col'=8] {'col'}, use_global_device_ids=true, to_apply=%region_10.11 | all-reduce | flops 3072 | bytes 24576 | tf_op jit(solution)/shard_map/psum | solution.py:81
  (85 shorter events, 108.3 us)
Async XLA Ops:
  7.2 163.6 %all-gather.6.cloned.1.call-start = ((), (), s32[]{:S(2)}) async-start(), calls=%async_computation | async-start | bytes 9437184 | tf_op jit(solution)/shard_map/all_gather | solution.py:67
  41.8 1.3 copy-start.4
  43.0 189.8 %all-reduce.7.cloned.1.call-start = ((), (), s32[]{:S(2)}) async-start(), calls=%async_computation.1 | async-start | bytes 4325376 | tf_op jit(solution)/shard_map/psum | solution.py:68
  51.6 0.8 copy-start.2
  64.1 8.5 copy-start
  182.0 177.9 %all-gather.8.cloned.1.call-start = ((), (), s32[]{:S(2)}) async-start(), calls=%async_computation.2 | async-start | bytes 9437184 | tf_op jit(solution)/shard_map/all_gather | solution.py:67
  190.4 42.4 %copy-start.3 = (f32[6,2048,8]{1,2,0:T(8,128)S(1)}, f32[6,2048,8]{1,2,0:T(8,128)}, u32[]{:S(2)}) copy-start(f32[6,2048,8]{1,2,0:T(8,128)} %copy-done.2) | copy-start | bytes 1179652
  190.4 272.5 %all-reduce.9.cloned.1.call-start = ((), (), s32[]{:S(2)}) async-start(), calls=%async_computation.3 | async-start | bytes 8519680 | tf_op jit(solution)/shard_map/psum | solution.py:68
  378.0 1.0 copy-start.1
  378.0 211.9 %all-gather.10.cloned.1.call-start = ((), (), s32[]{:S(2)}) async-start(), calls=%async_computation.4 | async-start | bytes 9437184 | tf_op jit(solution)/shard_map/all_gather | solution.py:67
  380.0 354.3 %all-reduce.11.cloned.1.call-start = ((), (), s32[]{:S(2)}) async-start(), calls=%async_computation.5 | async-start | bytes 12713984 | tf_op jit(solution)/shard_map/psum | solution.py:68
  615.3 246.2 %all-gather.12.cloned.1.call-start = ((), (), s32[]{:S(2)}) async-start(), calls=%async_computation.6 | async-start | bytes 9437184 | tf_op jit(solution)/shard_map/all_gather | solution.py:67
  623.2 422.1 %all-reduce.13.cloned.1.call-start = ((), (), s32[]{:S(2)}) async-start(), calls=%async_computation.7 | async-start | bytes 16908288 | tf_op jit(solution)/shard_map/psum | solution.py:68
  893.0 279.4 %all-gather.14.cloned.1.call-start = ((), (), s32[]{:S(2)}) async-start(), calls=%async_computation.8 | async-start | bytes 9437184 | tf_op jit(solution)/shard_map/all_gather | solution.py:67
  894.2 506.6 %all-reduce.15.cloned.1.call-start = ((), (), s32[]{:S(2)}) async-start(), calls=%async_computation.9 | async-start | bytes 21102592 | tf_op jit(solution)/shard_map/psum | solution.py:68
Sparse Core Ops, SparseCore 0:
  43.1 127.6 all-gather.5
  182.1 50.6 all-reduce.6
  234.9 124.9 all-gather.7
  378.1 84.7 all-reduce.8
  464.8 125.0 all-gather.9
  615.5 118.8 all-reduce.10
  736.4 125.1 all-gather.11
  893.2 152.0 all-reduce.12
  1047.4 125.0 all-gather.13
  1214.7 185.9 all-reduce.14
where the time goes:
time: 1490 us
  waiting for transfers between devices  1060 us (71%)
  matrix products  216 us (14%)
  other arithmetic  70.2 us (5%)
  local copies, waits for them, and re-layouts  61.6 us (4%)
  blocking collectives  46.2 us (3%)
  between operations  27.1 us (2%)
    psum x5, waiting for transfers between devices, body(): summed = lax.psum(partial_value, 'row')  564 us
    all_gather x5, waiting for transfers between devices, body(): lax.all_gather(blocks, 'col', axis=2, tiled=True)  499 us
    dot_general x5, matrix products, contract(): return jnp.einsum('tiw,tin->wn', panel_piece, selected, precision=HIGHEST)  128 us
    dot_general x6, matrix products, body(): jnp.dot(lower_inv[current_sup].T, right, precision=HIGHEST, preferred_ele...  88.2 us
    psum x1, blocking collectives, body(): variance = lax.psum(squares, 'col')  37.7 us
  transfers between devices with their start and end apart: 10, of which 10 were waited for; matrix products, arithmetic and copies ran while one was open for 9% of the time, Pallas kernels for 0%

commit v1 on v0

--- a/solution.py
+++ b/solution.py
@@ -64,7 +64,11 @@
                 )
             blocks = jnp.stack(picks)
             selected = jnp.stack(chosen_rows)
-            partial_value = contract(selected, lax.all_gather(blocks, "col", axis=2, tiled=True))
+
+            def measure_spans(vals, group_axis):
+                return jnp.concatenate(lax.all_gather(vals, axis_name=group_axis), axis=2)
+
+            partial_value = contract(selected, measure_spans(blocks, "col"))
             summed = lax.psum(partial_value, "row")
         split_at = summed.shape[1] - rhs_width
         remaining = jnp.concatenate(

time: 1490 us -> 1440 us (0.966)
  waiting for transfers between devices: 1060 us -> 925 us
  local copies, waits for them, and re-layouts: 61.6 us -> 156 us
    all_gather x5, waiting for transfers between devices: 499 us -> 405 us  [measure_spans(): return jnp.concatenate(lax.all_gather(vals, axis_name=group_axis), axis=2)]
    all_gather x0 -> x5, local copies, waits for them, and re-layouts: none -> 57.9 us  [measure_spans(): return jnp.concatenate(lax.all_gather(vals, axis_name=group_axis), axis=2)]
    reshape x0 -> x5, local copies, waits for them, and re-layouts: none -> 46.7 us  [measure_spans(): return jnp.concatenate(lax.all_gather(vals, axis_name=group_axis), axis=2)]
    psum x5, waiting for transfers between devices: 564 us -> 520 us  [body(): summed = lax.psum(partial_value, 'row')]
  transfers between devices with their start and end apart: 10 -> 10, of which waited for: 10 -> 10; matrix products, arithmetic and copies ran while one was open for 9% -> 20% of each run, Pallas kernels for 0% -> 0%
where the time goes in v1:
time: 1440 us; the launch traced here: 1430 us
  waiting for transfers between devices  925 us (64%)
  matrix products  204 us (14%)
  local copies, waits for them, and re-layouts  156 us (11%)
  other arithmetic  72.9 us (5%)
  blocking collectives  45.6 us (3%)
  between operations  27.4 us (2%)
    psum x5, waiting for transfers between devices, body(): summed = lax.psum(partial_value, 'row')  520 us
    all_gather x5, waiting for transfers between devices, measure_spans(): return jnp.concatenate(lax.all_gather(vals, axis_name=group_axis), axis=2)  405 us
    dot_general x5, matrix products, contract(): return jnp.einsum('tiw,tin->wn', panel_piece, selected, precision=HIGHEST)  116 us
    dot_general x6, matrix products, body(): jnp.dot(lower_inv[current_sup].T, right, precision=HIGHEST, preferred_ele...  88 us
    all_gather x5, local copies, waits for them, and re-layouts, measure_spans(): return jnp.concatenate(lax.all_gather(vals, axis_name=group_axis), axis=2)  57.9 us
    reshape x5, local copies, waits for them, and re-layouts, measure_spans(): return jnp.concatenate(lax.all_gather(vals, axis_name=group_axis), axis=2)  46.7 us
    psum x1, blocking collectives, body(): variance = lax.psum(squares, 'col')  37.7 us
  transfers between devices with their start and end apart: 10, of which 10 were waited for; matrix products, arithmetic and copies ran while one was open for 20% of the time, Pallas kernels for 0%

profile of v1, /device:TPU:0, one launch (start us, length us, event | category | flops | bytes accessed | tf_op | source)
XLA Modules:
  0.0 1431.6 jit_solution(7561066047648841683)
XLA Ops:
  15.8 15.3 %broadcast_multiply_fusion = f32[6,512,6,256]{3,1,2,0:T(8,128)} fusion(f32[6,512,6,256]{3,1,2,0:T(8,128)} %param.17, f32[6,512,6]{1,2,0:T(8,128)S(1)} %multiply_bitcast_fusion.10), kind=kLoop, calls=%fused_computation.18 | loop fusion | flops 4718592 | bytes 37822464 | tf_op jit(solution)/shard_map/mul | solution.py:36
  88.0 83.6 %all-gather.11.cloned.1.call-done = f32[16,512,256]{2,1,0:T(8,128)} async-done(((f32[2,512,256]{2,1,0:T(8,128)}), f32[16,512,256]{2,1,0:T(8,128)}) %all-gather.11.cloned.1.call-update) | async-done | bytes 8388624 | tf_op jit(solution)/shard_map/all_gather | solution.py:69
  215.1 81.3 %all-gather.13.cloned.1.call-done = f32[16,512,256]{2,1,0:T(8,128)} async-done(((f32[2,512,256]{2,1,0:T(8,128)}), f32[16,512,256]{2,1,0:T(8,128)}) %all-gather.13.cloned.1.call-update) | async-done | bytes 8388624 | tf_op jit(solution)/shard_map/all_gather | solution.py:69
  296.4 11.6 copy.33
  317.5 31.9 %all-reduce.7.cloned.1.call-done = f32[2048,264]{0,1:T(8,128)} async-done(((f32[2048,264]{0,1:T(8,128)}), f32[2048,264]{0,1:T(8,128)}) %all-reduce.7.cloned.1.call-update) | async-done | bytes 2162704 | tf_op jit(solution)/shard_map/psum | solution.py:72
  365.9 15.4 %convolution_bitcast_fusion.3 = f32[2048,520]{0,1:T(8,128)} fusion(f32[2,512,2048]{2,1,0:T(8,128)S(1)} %bitcast.220, f32[1,512,520]{1,2,0:T(8,128)S(1)} %slice_bitcast_fusion.38, f32[1,512,520]{1,2,0:T(8,128)S(1)} %slice_bitcast_fusion.39), kind=kOutput, calls=%fused_computation.62 | convolution fusion | flops 13086760960 | bytes 14778368 | tf_op jit(solution)/shard_map/tiw,tin->wn/dot_general | solution.py:11
  389.5 86.5 %all-gather.15.cloned.1.call-done = f32[16,512,256]{2,1,0:T(8,128)} async-done(((f32[2,512,256]{2,1,0:T(8,128)}), f32[16,512,256]{2,1,0:T(8,128)}) %all-gather.15.cloned.1.call-update) | async-done | bytes 8388624 | tf_op jit(solution)/shard_map/all_gather | solution.py:69
  476.0 11.6 copy.32
  496.9 66.1 %all-reduce.9.cloned.1.call-done = f32[2048,520]{0,1:T(8,128)} async-done(((f32[2048,520]{0,1:T(8,128)}), f32[2048,520]{0,1:T(8,128)}) %all-reduce.9.cloned.1.call-update) | async-done | bytes 4259856 | tf_op jit(solution)/shard_map/psum | solution.py:72
  566.4 13.0 bitcast_dynamic-update-slice_fusion
  583.5 22.7 %convolution_bitcast_fusion.2 = f32[2048,776]{0,1:T(8,128)} fusion(f32[2,512,2048]{2,1,0:T(8,128)S(1)} %bitcast.222, f32[1,512,776]{1,2,0:T(8,128)S(1)} %slice_bitcast_fusion.28, f32[1,512,776]{1,2,0:T(8,128)S(1)} %slice_bitcast_fusion.29), kind=kOutput, calls=%fused_computation.61 | convolution fusion | flops 19529474048 | bytes 17924096 | tf_op jit(solution)/shard_map/tiw,tin->wn/dot_general | solution.py:11
  607.6 82.0 %all-gather.17.cloned.1.call-done = f32[16,512,256]{2,1,0:T(8,128)} async-done(((f32[2,512,256]{2,1,0:T(8,128)}), f32[16,512,256]{2,1,0:T(8,128)}) %all-gather.17.cloned.1.call-update) | async-done | bytes 8388624 | tf_op jit(solution)/shard_map/all_gather | solution.py:69
  689.6 11.6 copy.31
  710.6 100.3 %all-reduce.11.cloned.1.call-done = f32[2048,776]{0,1:T(8,128)} async-done(((f32[2048,776]{0,1:T(8,128)}), f32[2048,776]{0,1:T(8,128)}) %all-reduce.11.cloned.1.call-update) | async-done | bytes 6357008 | tf_op jit(solution)/shard_map/psum | solution.py:72
  815.3 16.9 %fusion.53 = f32[6,512,1544]{1,2,0:T(8,128)} fusion(f32[6,512,1544]{1,2,0:T(8,128)} %bitcast_dynamic-update-slice_fusion, f32[2048,8]{0,1:T(8,128)S(1)} %slice_subtract_fusion.2, f32[2048,768]{0,1:T(8,128)S(1)} %slice_negate_fusion.2, f32[2048,256]{0,1:T(8,128)S(1)} %fusion.67, f32[6,2048,512]{2,1,0:T(8,128)} %copy-done), kind=kOutput, calls=%fused_computation.68 | convolution fusion | flops 12989792256 | bytes 14761984 | tf_op jit(solution)/shard_map/dot_general | solution.py:78
  836.3 30.2 %convolution_bitcast_fusion.1 = f32[2048,1032]{0,1:T(8,128)} fusion(f32[2,512,2048]{2,1,0:T(8,128)S(1)} %bitcast.224, f32[1,512,1032]{1,2,0:T(8,128)S(1)} %slice_bitcast_fusion.26, f32[1,512,1032]{1,2,0:T(8,128)S(1)} %slice_bitcast_fusion.27), kind=kOutput, calls=%fused_computation.20 | convolution fusion | flops 25972187136 | bytes 21069824 | tf_op jit(solution)/shard_map/tiw,tin->wn/dot_general | solution.py:11
  866.5 71.2 %all-gather.19.cloned.1.call-done = f32[16,512,256]{2,1,0:T(8,128)} async-done(((f32[2,512,256]{2,1,0:T(8,128)}), f32[16,512,256]{2,1,0:T(8,128)}) %all-gather.19.cloned.1.call-update) | async-done | bytes 8388624 | tf_op jit(solution)/shard_map/all_gather | solution.py:69
  937.7 11.6 copy.30
  958.5 133.8 %all-reduce.13.cloned.1.call-done = f32[2048,1032]{0,1:T(8,128)} async-done(((f32[2048,1032]{0,1:T(8,128)}), f32[2048,1032]{0,1:T(8,128)}) %all-reduce.13.cloned.1.call-update) | async-done | bytes 8454160 | tf_op jit(solution)/shard_map/psum | solution.py:72
  1097.6 20.5 %fusion.41 = f32[6,512,1544]{1,2,0:T(8,128)} fusion(f32[6,512,1544]{1,2,0:T(8,128)} %fusion.53, f32[2048,8]{0,1:T(8,128)S(1)} %slice_subtract_fusion.1, f32[2048,1024]{0,1:T(8,128)S(1)} %slice_negate_fusion.1, f32[2048,256]{0,1:T(8,128)S(1)} %fusion.67, f32[6,2048,512]{2,1,0:T(8,128)} %copy-done), kind=kOutput, calls=%fused_computation.64 | convolution fusion | flops 16212066304 | bytes 17383424 | tf_op jit(solution)/shard_map/dot_general | solution.py:78
  1122.2 36.4 %convolution_bitcast_fusion = f32[2048,1288]{0,1:T(8,128)} fusion(f32[2,512,2048]{2,1,0:T(8,128)S(1)} %bitcast.226, f32[1,512,1288]{1,2,0:T(8,128)S(1)} %slice_bitcast_fusion.24, f32[1,512,1288]{1,2,0:T(8,128)S(1)} %slice_bitcast_fusion.25), kind=kOutput, calls=%fused_computation.19 | convolution fusion | flops 32414900224 | bytes 24215552 | tf_op jit(solution)/shard_map/tiw,tin->wn/dot_general | solution.py:11
  1158.6 188.1 %all-reduce.15.cloned.1.call-done = f32[2048,1288]{0,1:T(8,128)} async-done(((f32[2048,1288]{0,1:T(8,128)}), f32[2048,1288]{0,1:T(8,128)}) %all-reduce.15.cloned.1.call-update) | async-done | bytes 10551312 | tf_op jit(solution)/shard_map/psum | solution.py:72
  1352.7 23.9 %fusion.47 = f32[6,512,1544]{1,2,0:T(8,128)} fusion(f32[6,512,1544]{1,2,0:T(8,128)} %fusion.41, f32[2048,8]{0,1:T(8,128)S(1)} %slice_subtract_fusion, f32[2048,1280]{0,1:T(8,128)S(1)} %slice_negate_fusion, f32[2048,256]{0,1:T(8,128)S(1)} %fusion.67, f32[6,2048,512]{2,1,0:T(8,128)} %copy-done), kind=kOutput, calls=%fused_computation.66 | convolution fusion | flops 19434340352 | bytes 20004864 | tf_op jit(solution)/shard_map/dot_general | solution.py:78
  1386.9 37.7 %psum.47 = f32[6,512]{1,0:T(8,128)} all-reduce(f32[6,512]{1,0:T(8,128)S(1)} %fusion), channel_id=1, replica_groups=mesh['row'=4,'col'=8] {'col'}, use_global_device_ids=true, to_apply=%region_10.11 | all-reduce | flops 3072 | bytes 24576 | tf_op jit(solution)/shard_map/psum | solution.py:85
  (113 shorter events, 201.2 us)
Async XLA Ops:
  7.2 164.4 %all-gather.11.cloned.1.call-start = ((), (), s32[]{:S(2)}) async-start(), calls=%async_computation.5 | async-start | bytes 9437184 | tf_op jit(solution)/shard_map/all_gather | solution.py:69
  44.2 8.7 copy-start.3
  44.2 252.2 %all-gather.13.cloned.1.call-start = ((), (), s32[]{:S(2)}) async-start(), calls=%async_computation.6 | async-start | bytes 9437184 | tf_op jit(solution)/shard_map/all_gather | solution.py:69
  52.8 296.6 %all-reduce.7.cloned.1.call-start = ((), (), s32[]{:S(2)}) async-start(), calls=%async_computation | async-start | bytes 4325376 | tf_op jit(solution)/shard_map/psum | solution.py:72
  60.9 0.8 copy-start.1
  73.5 8.4 copy-start
  203.8 272.2 %all-gather.15.cloned.1.call-start = ((), (), s32[]{:S(2)}) async-start(), calls=%async_computation.7 | async-start | bytes 9437184 | tf_op jit(solution)/shard_map/all_gather | solution.py:69
  206.2 356.8 %all-reduce.9.cloned.1.call-start = ((), (), s32[]{:S(2)}) async-start(), calls=%async_computation.1 | async-start | bytes 8519680 | tf_op jit(solution)/shard_map/psum | solution.py:72
  308.0 41.4 %copy-start.2 = (f32[6,2048,8]{1,2,0:T(8,128)S(1)}, f32[6,2048,8]{1,2,0:T(8,128)}, u32[]{:S(2)}) copy-start(f32[6,2048,8]{1,2,0:T(8,128)} %copy-done.1) | copy-start | bytes 1179652
  352.1 13.6 slice-start
  361.9 4.0 slice-start.1
  381.4 308.3 %all-gather.17.cloned.1.call-start = ((), (), s32[]{:S(2)}) async-start(), calls=%async_computation.8 | async-start | bytes 9437184 | tf_op jit(solution)/shard_map/all_gather | solution.py:69
  389.0 421.8 %all-reduce.11.cloned.1.call-start = ((), (), s32[]{:S(2)}) async-start(), calls=%async_computation.2 | async-start | bytes 12713984 | tf_op jit(solution)/shard_map/psum | solution.py:72
  566.4 17.0 %slice-start.2 = ((s8[8388608]{0:T(1024)(128)(4,1)}), s8[4194304]{0:T(1024)(128)(4,1)S(1)}, s32[]{:S(2)}) async-start(s8[8388608]{0:T(1024)(128)(4,1)} %bitcast.221), calls=%async_computation.12 | async-start | bytes 8388608
  579.4 4.1 slice-start.3
  606.2 331.5 %all-gather.19.cloned.1.call-start = ((), (), s32[]{:S(2)}) async-start(), calls=%async_computation.9 | async-start | bytes 9437184 | tf_op jit(solution)/shard_map/all_gather | solution.py:69
  607.3 485.0 %all-reduce.13.cloned.1.call-start = ((), (), s32[]{:S(2)}) async-start(), calls=%async_computation.3 | async-start | bytes 16908288 | tf_op jit(solution)/shard_map/psum | solution.py:72
  811.7 24.5 %slice-start.4 = ((s8[8388608]{0:T(1024)(128)(4,1)}), s8[4194304]{0:T(1024)(128)(4,1)S(1)}, s32[]{:S(2)}) async-start(s8[8388608]{0:T(1024)(128)(4,1)} %bitcast.223), calls=%async_computation.14 | async-start | bytes 8388608
  815.3 20.9 %slice-start.5 = ((s8[8388608]{0:T(1024)(128)(4,1)}), s8[4194304]{0:T(1024)(128)(4,1)S(1)}, s32[]{:S(2)}) async-start(s8[8388608]{0:T(1024)(128)(4,1)} %bitcast.223), calls=%async_computation.15 | async-start | bytes 8388608
  866.4 480.3 %all-reduce.15.cloned.1.call-start = ((), (), s32[]{:S(2)}) async-start(), calls=%async_computation.4 | async-start | bytes 21102592 | tf_op jit(solution)/shard_map/psum | solution.py:72
  1093.2 29.0 %slice-start.6 = ((s8[8388608]{0:T(1024)(128)(4,1)}), s8[4194304]{0:T(1024)(128)(4,1)S(1)}, s32[]{:S(2)}) async-start(s8[8388608]{0:T(1024)(128)(4,1)} %bitcast.225), calls=%async_computation.16 | async-start | bytes 8388608
  1097.6 24.6 %slice-start.7 = ((s8[8388608]{0:T(1024)(128)(4,1)}), s8[4194304]{0:T(1024)(128)(4,1)S(1)}, s32[]{:S(2)}) async-start(s8[8388608]{0:T(1024)(128)(4,1)} %bitcast.225), calls=%async_computation.17 | async-start | bytes 8388608
Sparse Core Ops, SparseCore 0:
  44.4 127.1 all-gather.10
  173.7 122.6 all-gather.12
  298.8 50.6 all-reduce.6
  351.4 124.5 all-gather.14
  478.2 84.7 all-reduce.8
  565.0 124.5 all-gather.16
  692.0 118.8 all-reduce.10
  813.0 124.6 all-gather.18
  940.2 152.0 all-reduce.12
  1158.7 187.9 all-reduce.14
